TPU v7x, 32 devices: a whole 2x2x4 slice. The times are simulated.
32 devices in a mesh: dp: 4 (over z), seq: 2 (over core), tensor: 4 (over y, x).
Axes of the slice: x: 2, y: 2, z: 4, core: 2. Of those that a mesh axis runs over, the one named last changes fastest.
Arguments:
- block_input: bfloat16 [1024, 1024], P(('dp', 'seq')), may hold values from -6 to 6
- norm1_gain: float32 [1024], replicated, may hold values from 0.5 to 1.5
- q_weight: bfloat16 [1024, 768], replicated, may hold values from -0.1875 to 0.1875
- k_weight: bfloat16 [1024, 768], replicated, may hold values from -0.1875 to 0.1875
- v_weight: bfloat16 [1024, 6, 256], P(None, None, 'tensor'), may hold values from -0.1875 to 0.1875
- gate_weight: bfloat16 [1024, 6, 256], P(None, None, 'tensor'), may hold values from -0.1875 to 0.1875
- beta_weight: bfloat16 [1024, 6], replicated, may hold values from -0.1875 to 0.1875
- decay_weight: bfloat16 [1024, 6], replicated, may hold values from -0.1875 to 0.1875
- q_conv: float32 [4, 768], replicated, may hold values from -3 to 3
- k_conv: float32 [4, 768], replicated, may hold values from -3 to 3
- v_conv: float32 [4, 6, 256], P(None, None, 'tensor'), may hold values from -3 to 3
- decay_scale: float32 [6], replicated, may hold values from 0.0009765625 to 0.05
- dt_bias: float32 [6], replicated, may hold values from -1 to 1
- out_gain: float32 [256], P('tensor'), may hold values from 0.5 to 1.5
- out_weight: bfloat16 [6, 256, 1024], P(None, 'tensor'), may hold values from -0.3125 to 0.3125
- norm2_gain: float32 [1024], replicated, may hold values from 0.5 to 1.5
- ffn_gate: bfloat16 [1024, 2816], P(None, 'tensor'), may hold values from -0.1875 to 0.1875
- ffn_up: bfloat16 [1024, 2816], P(None, 'tensor'), may hold values from -0.1875 to 0.1875
- ffn_down: bfloat16 [2816, 1024], P('tensor'), may hold values from -0.109375 to 0.109375
- cotangent: bfloat16 [1024, 1024], P(('dp', 'seq')), may hold values from -6 to 6
Outputs:
- block_output: bfloat16 [1024, 1024], P(('dp', 'seq'))
- grad_input: float32 [1024, 1024], P(('dp', 'seq'))
- grad_norm1_gain: float32 [1024], replicated
- grad_q_weight: float32 [1024, 768], replicated
- grad_k_weight: float32 [1024, 768], replicated
- grad_v_weight: float32 [1024, 6, 256], P(None, None, 'tensor')
- grad_gate_weight: float32 [1024, 6, 256], P(None, None, 'tensor')
- grad_beta_weight: float32 [1024, 6], replicated
- grad_decay_weight: float32 [1024, 6], replicated
- grad_q_conv: float32 [4, 768], replicated
- grad_k_conv: float32 [4, 768], replicated
- grad_v_conv: float32 [4, 6, 256], P(None, None, 'tensor')
- grad_decay_scale: float32 [6], replicated
- grad_dt_bias: float32 [6], replicated
- grad_out_gain: float32 [256], P('tensor')
- grad_out_weight: float32 [6, 256, 1024], P(None, 'tensor')
- grad_norm2_gain: float32 [1024], replicated
- grad_ffn_gate: float32 [1024, 2816], P(None, 'tensor')
- grad_ffn_up: float32 [1024, 2816], P(None, 'tensor')
- grad_ffn_down: float32 [2816, 1024], P('tensor')
All inputs are finite; a program needn't handle non-finite values.
Results may differ from a plain program's by a relative error of at most 0.025.
Values may be sent and summed in bfloat16 or wider, within the bound.
No kernel may reach another device: no remote copies, remote signals or barrier semaphores. Data moves between devices by JAX's collectives and lax.ppermute only.
A program may use at most 128 MiB of HBM per device.

v0:
```python
import jax
import jax.numpy as jnp
from jax import lax
from jax.sharding import PartitionSpec as P

DV = 256
SPAN = 64
EPS = 1e-06
HIGH_PRECISION = lax.Precision.HIGHEST


def from_behind(value, axis, by):
    length = lax.axis_size(axis)
    pairs = [(i, i + by) for i in range(length) if 0 <= i + by < length]
    return lax.ppermute(value, axis, pairs)


def matmul(left, right):
    return jnp.dot(left, right, preferred_element_type=jnp.float32)


def rms_scale(matrix, gain):
    return matrix * lax.rsqrt(jnp.mean(matrix * matrix, axis=-1, keepdims=True) + EPS) * gain


def swiglu(gate_act, up_act):
    return jax.nn.silu(gate_act) * up_act


def conv_silu(edge_rows, rows, conv_taps):
    length = rows.shape[0]
    padded = jnp.concatenate([edge_rows, rows], axis=0)
    summed = conv_taps[0] * padded[0:length]
    for offset in range(1, conv_taps.shape[0]):
        summed = summed + conv_taps[offset] * padded[offset : offset + length]
    return jax.nn.silu(summed)


def unit_rows(matrix):
    return matrix * lax.rsqrt(jnp.sum(matrix * matrix, axis=-1, keepdims=True) + EPS)


def mixer_inputs(
    q_proj,
    k_proj,
    v_proj,
    b_proj,
    a_proj,
    q_edge,
    k_edge,
    v_edge,
    q_conv,
    k_conv,
    v_conv,
    decay_scale,
    dt_bias,
):
    length = q_proj.shape[0]
    n_heads = b_proj.shape[1]
    queries = conv_silu(q_edge, q_proj, q_conv).reshape(length, n_heads, -1)
    key_vecs = conv_silu(k_edge, k_proj, k_conv).reshape(length, n_heads, -1)
    values = conv_silu(v_edge, v_proj, v_conv.reshape(v_conv.shape[0], -1)).reshape(
        length, n_heads, -1
    )
    queries = unit_rows(queries) * queries.shape[2] ** (-0.5)
    key_vecs = unit_rows(key_vecs)
    beta_gate = jax.nn.sigmoid(b_proj)
    log_decay = -decay_scale * jax.nn.softplus(a_proj + dt_bias)
    return (
        jnp.transpose(queries, (1, 0, 2)),
        jnp.transpose(key_vecs, (1, 0, 2)),
        jnp.transpose(values, (1, 0, 2)),
        beta_gate.T,
        log_decay.T,
    )


def gated_norm(head_out, gate_proj, gain, sum_squares):
    scale_rows = lax.rsqrt(sum_squares / DV + EPS)[..., None]
    return head_out * scale_rows * gain * jax.nn.silu(gate_proj)


def delta_run(queries, key_vecs, values, beta_gate, log_decay, start_state):
    n_heads, length, key_width = key_vecs.shape
    val_width = values.shape[2]
    n_blocks = length // SPAN
    q_blk = queries.reshape(n_heads, n_blocks, SPAN, key_width)
    k_blk = key_vecs.reshape(n_heads, n_blocks, SPAN, key_width)
    v_blk = values.reshape(n_heads, n_blocks, SPAN, val_width)
    b_blk = beta_gate.reshape(n_heads, n_blocks, SPAN)
    g_cum = jnp.cumsum(log_decay.reshape(n_heads, n_blocks, SPAN), axis=-1)
    places = jnp.arange(SPAN)
    strict = places[:, None] > places[None, :]
    within = places[:, None] >= places[None, :]
    differ = g_cum[..., :, None] - g_cum[..., None, :]
    decays = jnp.where(within, jnp.exp(jnp.where(within, differ, 0.0)), 0.0)
    k_gram = jnp.einsum("hnik,hnjk->hnij", k_blk, k_blk, precision=HIGH_PRECISION)
    l_mat = jnp.eye(SPAN, dtype=jnp.float32) + jnp.where(
        strict, b_blk[..., :, None] * k_gram * decays, 0.0
    )
    right_side = jnp.concatenate(
        [b_blk[..., None] * v_blk, (b_blk * jnp.exp(g_cum))[..., None] * k_blk], axis=-1
    )
    solved = lax.linalg.triangular_solve(
        l_mat, right_side, left_side=True, lower=True, unit_diagonal=True
    )
    updates = solved[..., :val_width]
    w_mat = solved[..., val_width:]
    qk_mat = jnp.einsum("hnik,hnjk->hnij", q_blk, k_blk, precision=HIGH_PRECISION) * decays
    g_last = g_cum[..., -1:]
    k_end = k_blk * jnp.exp(g_last - g_cum)[..., None]
    q_dec = q_blk * jnp.exp(g_cum)[..., None]

    def advance(current_state, block_in):
        (
            current_update_rows,
            current_write_rows,
            current_query_decayed,
            current_query_key,
            current_key_edge,
            current_gate_log,
        ) = block_in
        fresh_value_rows = current_update_rows - jnp.einsum(
            "nsz,nzu->nsu", current_write_rows, current_state, precision=HIGH_PRECISION
        )
        block_result = jnp.einsum(
            "nsz,nzu->nsu", current_query_decayed, current_state, precision=HIGH_PRECISION
        ) + jnp.einsum(
            "zdn,znb->zdb", current_query_key, fresh_value_rows, precision=HIGH_PRECISION
        )
        following_state = jnp.exp(current_gate_log)[..., None] * current_state + jnp.einsum(
            "ozq,ozp->oqp", current_key_edge, fresh_value_rows, precision=HIGH_PRECISION
        )
        return (following_state, block_result)

    blocks_in = tuple(
        (jnp.moveaxis(member, 1, 0) for member in (updates, w_mat, q_dec, qk_mat, k_end, g_last))
    )
    final_state, outputs = lax.scan(advance, start_state, blocks_in)
    return (jnp.moveaxis(outputs, 0, 1).reshape(n_heads, length, val_width), final_state)


def on_device(
    block_input,
    norm1_gain,
    q_weight,
    k_weight,
    v_weight,
    gate_weight,
    beta_weight,
    decay_weight,
    q_conv,
    k_conv,
    v_conv,
    decay_scale,
    dt_bias,
    out_gain,
    out_weight,
    norm2_gain,
    ffn_gate,
    ffn_up,
    ffn_down,
    cotangent,
):
    length = block_input.shape[0]
    model_width = block_input.shape[1]
    n_heads = beta_weight.shape[1]
    qk_cols = q_weight.shape[1]
    key_width = qk_cols // n_heads
    value_part = v_weight.shape[2]
    edge_count = q_conv.shape[0] - 1
    inputs_f = block_input.astype(jnp.float32)
    normed1, pull_norm1 = jax.vjp(rms_scale, inputs_f, norm1_gain)
    normed1_b = normed1.astype(jnp.bfloat16)
    v_mat = v_weight.reshape(model_width, -1)
    g_mat = gate_weight.reshape(model_width, -1)
    q_proj = matmul(normed1_b, q_weight)
    k_proj = matmul(normed1_b, k_weight)
    v_proj = matmul(normed1_b, v_mat)
    gate_proj = matmul(normed1_b, g_mat).reshape(length, n_heads, value_part)
    b_proj = matmul(normed1_b, beta_weight)
    a_proj = matmul(normed1_b, decay_weight)
    tail_rows = jnp.concatenate(
        [
            q_proj[length - edge_count :],
            k_proj[length - edge_count :],
            v_proj[length - edge_count :],
        ],
        axis=1,
    )
    edge_rows = from_behind(tail_rows, "seq", 1)
    prepared, pull_inputs = jax.vjp(
        mixer_inputs,
        q_proj,
        k_proj,
        v_proj,
        b_proj,
        a_proj,
        edge_rows[:, :qk_cols],
        edge_rows[:, qk_cols : 2 * qk_cols],
        edge_rows[:, 2 * qk_cols :],
        q_conv,
        k_conv,
        v_conv,
        decay_scale,
        dt_bias,
    )
    queries, key_vecs, values, beta_gate, log_decay = prepared
    empty_state = jnp.zeros((n_heads, key_width, value_part), jnp.float32)
    start_state = empty_state
    unused, end_state = delta_run(queries, key_vecs, values, beta_gate, log_decay, start_state)
    start_state = from_behind(end_state.astype(jnp.bfloat16), "seq", 1).astype(end_state.dtype)
    (mixed_heads, final_state), pull_delta = jax.vjp(
        delta_run, queries, key_vecs, values, beta_gate, log_decay, start_state
    )
    head_out = jnp.transpose(mixed_heads, (1, 0, 2))
    sum_squares = lax.psum(jnp.sum(head_out * head_out, axis=2), "tensor")
    gated, pull_gate = jax.vjp(gated_norm, head_out, gate_proj, out_gain, sum_squares)
    gated_b = gated.astype(jnp.bfloat16).reshape(length, -1)
    o_mat = out_weight.reshape(-1, model_width)
    mixer_total = lax.psum(matmul(gated_b, o_mat).astype(jnp.bfloat16), "tensor").astype(
        jnp.float32
    )
    hidden_res = inputs_f + mixer_total
    normed2, pull_norm2 = jax.vjp(rms_scale, hidden_res, norm2_gain)
    normed2_b = normed2.astype(jnp.bfloat16)
    inner, pull_ffn = jax.vjp(swiglu, matmul(normed2_b, ffn_gate), matmul(normed2_b, ffn_up))
    inner_b = inner.astype(jnp.bfloat16)
    ffn_total = lax.psum(matmul(inner_b, ffn_down).astype(jnp.bfloat16), "tensor").astype(
        jnp.float32
    )
    block_output = (hidden_res + ffn_total).astype(jnp.bfloat16)
    grad_inner = matmul(cotangent, ffn_down.T)
    grad_down = matmul(inner_b.T, cotangent)
    grad_gate_act, grad_up_act = pull_ffn(grad_inner)
    gate_grad_b = grad_gate_act.astype(jnp.bfloat16)
    up_grad_b = grad_up_act.astype(jnp.bfloat16)
    grad_ffn_gate = matmul(normed2_b.T, gate_grad_b)
    grad_ffn_up = matmul(normed2_b.T, up_grad_b)
    normed2_part = matmul(gate_grad_b, ffn_gate.T) + matmul(up_grad_b, ffn_up.T)
    grad_normed2 = lax.psum(normed2_part.astype(jnp.bfloat16), "tensor").astype(jnp.float32)
    grad_hidden_n, grad_norm2 = pull_norm2(grad_normed2)
    grad_hidden = cotangent.astype(jnp.float32) + grad_hidden_n
    grad_hidden_b = grad_hidden.astype(jnp.bfloat16)
    grad_gated = matmul(grad_hidden_b, o_mat.T).reshape(length, n_heads, value_part)
    grad_out_weight = matmul(gated_b.T, grad_hidden_b).reshape(out_weight.shape)
    heads_local, grad_gate_proj, grad_out_gain, squares_local = pull_gate(grad_gated)
    grad_squares = lax.psum(squares_local, "tensor")
    grad_heads = heads_local + 2.0 * head_out * grad_squares[..., None]
    grad_mixed = jnp.transpose(grad_heads, (1, 0, 2))
    end_grad = empty_state
    hop_terms = pull_delta((grad_mixed, end_grad))
    end_grad = from_behind(hop_terms[5].astype(jnp.bfloat16), "seq", -1).astype(jnp.float32)
    full_terms = pull_delta((grad_mixed, end_grad))
    delta_grads = tuple((full_terms[member] for member in range(5)))
    input_grads = pull_inputs(delta_grads)
    edge_grads = jnp.concatenate([input_grads[5], input_grads[6], input_grads[7]], axis=1)
    edge_back = from_behind(edge_grads, "seq", -1)
    q_grad_rows = input_grads[0].at[length - edge_count :].add(edge_back[:, :qk_cols])
    k_grad_rows = input_grads[1].at[length - edge_count :].add(edge_back[:, qk_cols : 2 * qk_cols])
    v_grad_rows = input_grads[2].at[length - edge_count :].add(edge_back[:, 2 * qk_cols :])
    qg_b = q_grad_rows.astype(jnp.bfloat16)
    kg_b = k_grad_rows.astype(jnp.bfloat16)
    vg_b = v_grad_rows.astype(jnp.bfloat16)
    bg_b = input_grads[3].astype(jnp.bfloat16)
    ag_b = input_grads[4].astype(jnp.bfloat16)
    gg_b = grad_gate_proj.reshape(length, -1).astype(jnp.bfloat16)
    normed1_part = (
        matmul(qg_b, q_weight.T)
        + matmul(kg_b, k_weight.T)
        + matmul(vg_b, v_mat.T)
        + matmul(gg_b, g_mat.T)
        + matmul(bg_b, beta_weight.T)
        + matmul(ag_b, decay_weight.T)
    )
    grad_input_n, grad_norm1 = pull_norm1(normed1_part)
    grad_input = grad_hidden + lax.psum(grad_input_n.astype(jnp.bfloat16), "tensor").astype(
        jnp.float32
    )
    shared = lax.psum(
        (
            grad_norm1,
            matmul(normed1_b.T, qg_b),
            matmul(normed1_b.T, kg_b),
            matmul(normed1_b.T, bg_b),
            matmul(normed1_b.T, ag_b),
            input_grads[8],
            input_grads[9],
            input_grads[11],
            input_grads[12],
        ),
        ("dp", "seq", "tensor"),
    )
    value_grad = matmul(normed1_b.T, vg_b).reshape(v_weight.shape)
    gate_grad = matmul(normed1_b.T, gg_b).reshape(gate_weight.shape)
    split = (
        lax.psum(value_grad.astype(jnp.bfloat16), ("dp", "seq")).astype(jnp.float32),
        lax.psum(gate_grad.astype(jnp.bfloat16), ("dp", "seq")).astype(jnp.float32),
        lax.psum(input_grads[10].astype(jnp.bfloat16), ("dp", "seq")).astype(jnp.float32),
        lax.psum(grad_out_gain.astype(jnp.bfloat16), ("dp", "seq")).astype(jnp.float32),
        lax.psum(grad_out_weight.astype(jnp.bfloat16), ("dp", "seq")).astype(jnp.float32),
        lax.psum(grad_norm2.astype(jnp.bfloat16), ("dp", "seq")).astype(jnp.float32),
        lax.psum(grad_ffn_gate.astype(jnp.bfloat16), ("dp", "seq")).astype(jnp.float32),
        lax.psum(grad_ffn_up.astype(jnp.bfloat16), ("dp", "seq")).astype(jnp.float32),
        lax.psum(grad_down.astype(jnp.bfloat16), ("dp", "seq")).astype(jnp.float32),
    )
    return (
        block_output,
        grad_input,
        shared[0],
        shared[1],
        shared[2],
        split[0],
        split[1],
        shared[3],
        shared[4],
        shared[5],
        shared[6],
        split[2],
        shared[7],
        shared[8],
        split[3],
        split[4],
        split[5],
        split[6],
        split[7],
        split[8],
    )


def solution(mesh):
    placed = (
        P(("dp", "seq"), None),
        P(),
        P(),
        P(),
        P(None, None, "tensor"),
        P(None, None, "tensor"),
        P(),
        P(),
        P(),
        P(),
        P(None, None, "tensor"),
        P(),
        P(),
        P("tensor"),
        P(None, "tensor", None),
        P(),
        P(None, "tensor"),
        P(None, "tensor"),
        P("tensor", None),
        P(("dp", "seq"), None),
    )
    return jax.shard_map(
        on_device,
        mesh=mesh,
        in_specs=placed,
        out_specs=(
            P(("dp", "seq"), None),
            P(("dp", "seq"), None),
            P(),
            P(),
            P(),
            P(None, None, "tensor"),
            P(None, None, "tensor"),
            P(),
            P(),
            P(),
            P(),
            P(None, None, "tensor"),
            P(),
            P(),
            P("tensor"),
            P(None, "tensor", None),
            P(),
            P(None, "tensor"),
            P(None, "tensor"),
            P("tensor", None),
        ),
        check_vma=False,
    )
```

profile of v0, /device:TPU:0, one launch (start us, length us, event | category | flops | bytes accessed | tf_op | source)
XLA Modules:
  0.0 872.2 jit_solution(6370596105471412092)
XLA Ops:
  13.4 2.4 collective-permute-start
  16.8 1.4 reduce_window_sum.24
  27.3 59.7 %custom-call.11 = f32[6,2,1,64,64]{3,4,2,1,0:T(8,128)S(1)} custom-call(f32[6,2,1,64,64]{4,3,2,1,0:T(8,128)} %get-tuple-element.1082), custom_call_target="InvertDiagBlocksLowerTriangular" | custom-call | tf_op jit(solution)/shard_map/triangular_solve/custom-call.1 | solution.py:104
  88.1 2.0 fusion.103
  91.2 2.0 while.77
  93.8 1.9 collective-permute-start.1
  95.8 2.7 fusion.145
  101.2 1.9 copy.179
  103.2 2.7 bitcast_multiply_fusion.11
  109.3 9.7 %while.75 = (s32[]{:T(128)}, f32[6,128,64]{1,2,0:T(8,128)S(1)}, f32[2,6,64,64]{3,2,1,0:T(8,128)}, f32[2,6,128,64]{2,3,1,0:T(8,128)}, f32[2,6,64,64]{3,2,1,0:T(8,...) while((s32[]{:T(128)}, f32[6,128,64]{1,2,0:T(8,128)S(1)}, ...), condition=%wide.region_7.9_spmd, body=%wide.region_6.8_spmd.sunk | while | flops 132268032 | bytes 5707657 | solution.py:139
  119.6 1.9 copy.188
  122.8 10.7 %psum.168 = f32[128,6]{0,1:T(8,128)S(1)} all-reduce(f32[128,6]{0,1:T(8,128)S(1)} %fusion.174), channel_id=1, replica_groups=mesh['dp'=4,'seq'=2,'tensor'=4] {'tensor'}, use_global_device_ids=true, to_apply=%region_9.11 | all-reduce | flops 768 | bytes 6144 | tf_op jit(solution)/shard_map/psum | solution.py:217
  134.7 2.2 multiply_convert_fusion.3
  138.5 1.9 copy.193
  140.4 40.1 %all-reduce.39.cloned.1.call-done = bf16[128,1024]{1,0:T(8,128)(2,1)} async-done(((bf16[128,1024]{1,0:T(8,128)(2,1)}), bf16[128,1024]{1,0:T(8,128)(2,1)}) %all-reduce.39.cloned.1.call-update) | async-done | bytes 262160 | tf_op jit(solution)/shard_map/psum | solution.py:221
  182.9 2.0 fusion.242
  187.3 1.6 convolution_convert_fusion.1
  190.0 1.6 convolution_convert_fusion
  192.8 2.7 convolution_convert_fusion.2
  195.5 40.5 %all-reduce.41.cloned.1.call-done = bf16[128,1024]{1,0:T(8,128)(2,1)} async-done(((bf16[128,1024]{1,0:T(8,128)(2,1)}), bf16[128,1024]{1,0:T(8,128)(2,1)}) %all-reduce.41.cloned.1.call-update) | async-done | bytes 262160 | tf_op jit(solution)/shard_map/psum | solution.py:241
  236.0 1.9 fusion.120
  240.0 1.7 multiply_reduce_fusion.14
  242.3 8.9 %psum.172 = f32[128,6]{0,1:T(8,128)S(1)} all-reduce(f32[128,6]{0,1:T(8,128)S(1)} %get-tuple-element.1089), channel_id=1, replica_groups=mesh['dp'=4,'seq'=2,'tensor'=4] {'tensor'}, use_global_device_ids=true, to_apply=%region_16.18 | all-reduce | flops 768 | bytes 6144 | tf_op jit(solution)/shard_map/psum | solution.py:248
  254.3 8.5 while.78
  264.2 2.3 convolution_bitcast_fusion.4
  270.4 20.2 %while.76 = (s32[]{:T(128)}, f32[6,128,64]{1,2,0:T(8,128)S(1)}, f32[2,6,64,64]{3,2,1,0:T(8,128)}, f32[2,6,64,128]{3,2,1,0:T(8,128)}, f32[2,6,64,128]{3,2,0,1:T(8...) while((s32[]{:T(128)}, f32[6,128,64]{1,2,0:T(8,128)S(1)}, ...), condition=%wide.region_21.23_spmd, body=%wide.region_19.22_spmd.sunk | while | flops 264560640 | bytes 16820268 | solution.py:139
  271.6 2.0 fusion.394
  277.6 1.6 fusion.392
  281.6 1.9 fusion.394
  287.6 1.6 fusion.392
  291.2 2.3 fusion.111
  295.9 2.4 multiply_reduce_fusion.10
  299.4 1.4 convolution_add_fusion.14
  302.8 1.5 add_add_fusion.2
  304.3 2.0 copy.214
  306.2 1.7 convolution_add_fusion.17
  310.0 1.8 add_add_fusion.3
  313.0 2.6 multiply_reduce_fusion.3
  321.8 2.1 multiply_reduce_fusion.17
  327.5 1.8 fusion.229
  333.4 1.5 add_add_fusion.4
  336.9 4.0 reduce_window_sum.25
  341.0 2.1 fusion.231
  344.4 1.7 split.35
  346.0 1.7 split.32
  349.1 1.5 scatter-add.11
  350.6 2.4 fusion.247
  354.3 2.6 convolution_add_fusion.13
  359.1 1.8 fusion.94
  371.1 2.3 fusion.248
  373.4 2.3 fusion.246
  376.5 30.4 %all-reduce.29 = (bf16[4,6,64]{2,1,0:T(8,128)(2,1)S(1)}, bf16[64]{0:T(256)(128)(2,1)S(1)}, bf16[1024]{0:T(1024)(128)(2,1)S(1)}) all-reduce(bf16[4,6,64]{2,1,0:T(8,128)(2,1)S(1)} %convert_element_type.192, bf16[64]{0:T(256)(128)(2,1)S(1)} %copy-done.180, ...), channel_id=1, replica_groups=mesh['dp'=4,'seq'=2,'tensor'=4] {'dp','seq'}, use_global_device_ids=true, to_apply=%region_57.59 | all-reduce | flops 2624 | bytes 10496 | tf_op jit(solution)/shard_map/psum | solution.py:299
  408.6 1.4 all-reduce.49.cloned.1.call-done
  410.0 1.8 add_convert_fusion
  411.8 1.8 convert_add_fusion.1
  413.6 144.4 %all-reduce.47.cloned.1.call-done = (bf16[1024,6,64]{0,2,1:T(8,128)(2,1)}, bf16[1024,6,64]{0,2,1:T(8,128)(2,1)}, bf16[6,64,1024]{2,1,0:T(8,128)(2,1)}, bf16[1024...) async-done(((bf16[1024,6,64]{0,2,1:T(8,128)(2,1)}, bf16[1024,6,64]{0,2,1:T(8,128)(2,1)}, bf16[6,64,1024]{2,1,0:T(8,128)(2,1)}, ...) | async-done | bytes 6684688 | tf_op jit(solution)/shard_map/psum | solution.py:297
  558.1 2.5 convert_element_type.187
  563.8 1.9 convert_element_type.201
  565.8 1.9 convert_element_type.203
  567.7 1.9 convert_element_type.205
  569.7 121.7 %all-reduce.43.cloned.1.call-done = (f32[1024]{0:T(1024)}, f32[1024,6]{0,1:T(8,128)}, f32[1024,6]{0,1:T(8,128)}, f32[4,768]{1,0:T(4,128)}, f32[4,768]{1,0:T(4,128)}, /*index=5*/f32[6]{0:T(128)}, f32[6]{0:T(128)}) async-done(((f32[1024]{0:T(1024)}, f32[1024,6]{0,1:T(8,128)}, f32[1024,6]{0,1:T(8,128)}, f32[4,768]{1,0:T(4,128)}, f32[4,768]{1,0:T(4,128)}, /*index=5*/f32[6]{0:T(128)}, f32[6]{0:T(128)}), ...) | async-done | bytes 77888 | tf_op jit(solution)/shard_map/psum | solution.py:280
  691.4 163.4 %all-reduce.45.cloned.1.call-done = (f32[1024,768]{1,0:T(8,128)}, f32[1024,768]{1,0:T(8,128)}) async-done(((f32[1024,768]{1,0:T(8,128)}, f32[1024,768]{1,0:T(8,128)}), (f32[1024,768]{1,0:T(8,128)}, f32[1024,768]{1,0:T(8,128)})) %all-reduce.45.cloned.1.call-update) | async-done | bytes 6291472 | tf_op jit(solution)/shard_map/psum | solution.py:280
  856.1 3.9 copy.411
  860.0 1.7 copy.412
  (645 shorter events, 130.8 us)
Async XLA Ops:
  7.2 173.3 %all-reduce.39.cloned.1.call-start = ((), (), s32[]{:S(2)}) async-start(), calls=%async_computation | async-start | bytes 524288 | tf_op jit(solution)/shard_map/psum | solution.py:221
  10.6 7.7 copy-start.1
  11.0 10.9 %copy-start.39 = (f32[128,768]{1,0:T(8,128)}, f32[128,768]{1,0:T(8,128)S(1)}, u32[]{:S(2)}) copy-start(f32[128,768]{1,0:T(8,128)S(1)} %fusion.239) | copy-start | bytes 1179652
  11.0 4.8 copy-start.183
  11.1 4.9 copy-start.147
  11.1 4.9 copy-start.184
  11.5 13.4 %copy-start.70 = (f32[128,384]{1,0:T(8,128)}, f32[128,384]{1,0:T(8,128)S(1)}, u32[]{:S(2)}) copy-start(f32[128,384]{1,0:T(8,128)S(1)} %fusion.240) | copy-start | bytes 589828
  11.5 6.8 copy-start.104
  11.5 7.3 copy-start.159
  11.5 7.4 copy-start.160
  12.3 6.7 copy-start.161
  13.4 7.9 collective-permute-start
  18.5 5.4 copy-start.130
  18.6 7.5 copy-start.91
  18.8 5.1 copy-start.120
  18.8 5.1 copy-start.122
  18.8 5.1 copy-start.124
  18.9 5.1 copy-start.126
  19.0 7.2 copy-start.100
  20.3 5.8 copy-start.102
  26.1 61.9 %copy-start.45 = (f32[6,128,64]{2,1,0:T(8,128)}, f32[6,128,64]{2,1,0:T(8,128)S(1)}, u32[]{:S(2)}) copy-start(f32[6,128,64]{2,1,0:T(8,128)S(1)} %copy.172) | copy-start | bytes 589828
  91.1 4.6 copy-start.98
  91.1 4.6 copy-start.112
  91.2 4.6 copy-start.114
  91.2 4.6 copy-start.116
  91.2 4.6 copy-start.118
  93.8 13.0 %collective-permute-start.1 = (bf16[6,128,64]{1,2,0:T(8,128)(2,1)}, bf16[6,128,64]{1,2,0:T(8,128)(2,1)}, u32[]{:S(2)}, u32[]{:S(2)}) collective-permute-start(bf16[6,128,64]{1,2,0:T(8,128)(2,1)} %convert_element_type.159), channel_id=1, source_target_pairs={{0,4},{1,5},{2,6},{3,7},{8,12},{9,13},{10,14},{11,15},{16,20},{17,... | collective-permute-start | bytes 294920 | tf_op jit(solution)/shard_map/ppermute | solution.py:15
  99.7 6.2 copy-start.10
  119.0 15.7 %copy-start.2 = (bf16[128,1024]{1,0:T(8,128)(2,1)S(1)}, bf16[128,1024]{1,0:T(8,128)(2,1)}, u32[]{:S(2)}) copy-start(bf16[128,1024]{1,0:T(8,128)(2,1)} %copy-done.1) | copy-start | bytes 786436
  119.0 15.7 %copy-start.181 = (f32[64]{0:T(128)S(1)}, f32[64]{0:T(128)}, u32[]{:S(2)}) copy-start(f32[64]{0:T(128)} %param.49) | copy-start | bytes 772
  136.9 46.0 %copy-start.87 = (bf16[128,6,64]{0,2,1:T(8,128)(2,1)}, bf16[128,6,64]{0,2,1:T(8,128)(2,1)S(1)}, u32[]{:S(2)}) copy-start(bf16[128,6,64]{0,2,1:T(8,128)(2,1)S(1)} %get-tuple-element.1094) | copy-start | bytes 294916
  136.9 43.6 %copy-start.4 = (bf16[128,1024]{1,0:T(8,128)(2,1)S(1)}, bf16[128,1024]{1,0:T(8,128)(2,1)}, u32[]{:S(2)}) copy-start(bf16[128,1024]{1,0:T(8,128)(2,1)} %param.36) | copy-start | bytes 786436
  136.9 44.9 %copy-start.110 = (f32[1024]{0:T(1024)S(1)}, f32[1024]{0:T(1024)}, u32[]{:S(2)}) copy-start(f32[1024]{0:T(1024)} %param.51) | copy-start | bytes 12292
  138.0 98.0 %all-reduce.41.cloned.1.call-start = ((), (), s32[]{:S(2)}) async-start(), calls=%async_computation.1 | async-start | bytes 524288 | tf_op jit(solution)/shard_map/psum | solution.py:241
  180.5 4.4 copy-start.34
  192.7 217.3 %all-reduce.49.cloned.1.call-start = ((), (), s32[]{:S(2)}) async-start(), calls=%async_computation.5 | async-start | bytes 1048576 | tf_op jit(solution)/shard_map/psum | solution.py:229
  236.0 4.1 copy-start.174
  236.0 4.1 copy-start.182
  239.3 12.0 %copy-start.95 = (f32[128,6,64]{0,2,1:T(8,128)S(1)}, f32[128,6,64]{0,2,1:T(8,128)}, u32[]{:S(2)}) copy-start(f32[128,6,64]{0,2,1:T(8,128)} %get-tuple-element.1095) | copy-start | bytes 589828
  254.3 9.9 %copy-start.89 = (bf16[128,6,64]{0,2,1:T(8,128)(2,1)S(1)}, bf16[128,6,64]{0,2,1:T(8,128)(2,1)}, u32[]{:S(2)}) copy-start(bf16[128,6,64]{0,2,1:T(8,128)(2,1)} %get-tuple-element.1055) | copy-start | bytes 294916
  262.9 3.6 collective-permute-start.2
  270.4 4.9 copy-start.6
  270.5 4.9 copy-start.54
  280.5 4.9 copy-start.6
  280.5 4.9 copy-start.54
  304.3 4.6 copy-start.11
  308.8 4.1 copy-start.40
  308.8 4.1 copy-start.42
  321.8 7.4 copy-start.97
  321.8 7.4 copy-start.108
  321.8 11.6 %copy-start.93 = (f32[6,2,64]{2,1,0:T(2,128)S(1)}, f32[6,2,64]{2,1,0:T(2,128)}, u32[]{:S(2)}) copy-start(f32[6,2,64]{2,1,0:T(2,128)} %copy-done.91) | copy-start | bytes 9220
  324.7 23.6 %copy-start.19 = (f32[128,768]{1,0:T(8,128)S(1)}, f32[128,768]{1,0:T(8,128)}, u32[]{:S(2)}) copy-start(f32[128,768]{1,0:T(8,128)} %copy-done.18) | copy-start | bytes 1179652
  324.7 23.6 %copy-start.21 = (f32[128,768]{1,0:T(8,128)S(1)}, f32[128,768]{1,0:T(8,128)}, u32[]{:S(2)}) copy-start(f32[128,768]{1,0:T(8,128)} %copy-done.20) | copy-start | bytes 1179652
  326.2 22.2 %collective-permute-start.3 = (f32[3,1920]{1,0:T(4,128)}, f32[3,1920]{1,0:T(4,128)}, u32[]{:S(2)}, u32[]{:S(2)}) collective-permute-start(f32[3,1920]{1,0:T(4,128)} %pad_maximum_fusion.4), channel_id=1, source_target_pairs={{4,0},{5,1},{6,2},{7,3},{12,8},{13,9},{14,10},{15,11},{20,16},{21,... | collective-permute-start | bytes 69128 | tf_op jit(solution)/shard_map/ppermute | solution.py:15
  341.0 7.4 copy-start.23
  341.0 7.4 copy-start.25
  341.0 7.4 copy-start.27
  349.1 5.2 copy-start.29
  363.1 194.9 %all-reduce.47.cloned.1.call-start = ((), (), s32[]{:S(2)}) async-start(), calls=%async_computation.4 | async-start | bytes 13369344 | tf_op jit(solution)/shard_map/psum | solution.py:297
  367.1 324.3 %all-reduce.43.cloned.1.call-start = ((), (), s32[]{:S(2)}) async-start(), calls=%async_computation.2 | async-start | bytes 190464 | tf_op jit(solution)/shard_map/psum | solution.py:280
  373.4 481.5 %all-reduce.45.cloned.1.call-start = ((), (), s32[]{:S(2)}) async-start(), calls=%async_computation.3 | async-start | bytes 12582912 | tf_op jit(solution)/shard_map/psum | solution.py:280
  375.7 34.3 %copy-start.17 = (bf16[128,1024]{1,0:T(8,128)(2,1)S(1)}, bf16[128,1024]{1,0:T(8,128)(2,1)}, u32[]{:S(2)}) copy-start(bf16[128,1024]{1,0:T(8,128)(2,1)} %all-reduce.39.cloned.1.call-done) | copy-start | bytes 786436
  860.0 4.1 copy-start.186
  860.0 4.6 copy-start.185
  (152 other events, 338.9 us)
Sparse Core Ops, SparseCore 0:
  138.1 42.4 all-reduce.38
  192.9 43.0 all-reduce.40
  363.2 46.7 all-reduce.48
  414.5 143.5 all-reduce.46
  565.5 125.8 all-reduce.42
  697.6 157.1 all-reduce.44
where the time goes:
time: 883 us; the launch traced here: 872 us
  waiting for transfers between devices  512 us (58%)
  other arithmetic  132 us (15%)
  matrix products  86.7 us (10%)
  local copies, waits for them, and re-layouts  66.9 us (8%)
  blocking collectives  50.1 us (6%)
  between operations  16.5 us (2%)
    psum x2, waiting for transfers between devices, on_device(): lax.psum((grad_norm1, matmul(normed1_b.T, qg_b), matmul(normed1_b.T, kg_b...  285 us
    psum x1, waiting for transfers between devices, on_device(): lax.psum(value_grad.astype(jnp.bfloat16), ('dp', 'seq')).astype(jnp.float32)  144 us
    another operation x5, other arithmetic, delta_run(): lax.linalg.triangular_solve(l_mat, right_side, left_side=True, lower=True...  61 us
    psum x1, waiting for transfers between devices, on_device(): lax.psum(normed2_part.astype(jnp.bfloat16), 'tensor').astype(jnp.float32)  40.5 us
    psum x1, waiting for transfers between devices, on_device(): lax.psum(matmul(gated_b, o_mat).astype(jnp.bfloat16), 'tensor')  40.1 us
    dot_general x30, matrix products, matmul(): return jnp.dot(left, right, preferred_element_type=jnp.float32)  38.7 us
    psum x1, blocking collectives, on_device(): lax.psum(input_grads[10].astype(jnp.bfloat16), ('dp', 'seq'))  30.4 us
    unnamed x363, local copies, waits for them, and re-layouts  25.5 us
  transfers between devices with their start and end apart: 10, of which 6 were waited for; matrix products, arithmetic and copies ran while one was open for 8% of the time, Pallas kernels for 0%

commit v1 on v0

--- a/solution.py
+++ b/solution.py
@@ -294,7 +294,9 @@
     value_grad = matmul(normed1_b.T, vg_b).reshape(v_weight.shape)
     gate_grad = matmul(normed1_b.T, gg_b).reshape(gate_weight.shape)
     split = (
-        lax.psum(value_grad.astype(jnp.bfloat16), ("dp", "seq")).astype(jnp.float32),
+        jnp.sum(lax.all_gather(value_grad.astype(jnp.bfloat16), ("dp", "seq")), axis=0).astype(
+            jnp.float32
+        ),
         lax.psum(gate_grad.astype(jnp.bfloat16), ("dp", "seq")).astype(jnp.float32),
         lax.psum(input_grads[10].astype(jnp.bfloat16), ("dp", "seq")).astype(jnp.float32),
         lax.psum(grad_out_gain.astype(jnp.bfloat16), ("dp", "seq")).astype(jnp.float32),

time: 883 us -> 932 us (1.055)
  waiting for transfers between devices: 512 us -> 555 us
    all_gather x0 -> x1, waiting for transfers between devices: none -> 56.1 us  [on_device(): lax.all_gather(value_grad.astype(jnp.bfloat16), ('dp', 'seq'))]
    psum x1, waiting for transfers between devices: 144 us -> 129 us  [on_device(): lax.psum(gate_grad.astype(jnp.bfloat16), ('dp', 'seq')).astype(jnp.float32)]
  transfers between devices with their start and end apart: 10 -> 11, of which waited for: 6 -> 6; matrix products, arithmetic and copies ran while one was open for 8% -> 8% of each run, Pallas kernels for 0% -> 0%
where the time goes in v1:
time: 932 us; the launch traced here: 921 us
  waiting for transfers between devices  555 us (60%)
  other arithmetic  136 us (15%)
  matrix products  87.8 us (9%)
  local copies, waits for them, and re-layouts  66.5 us (7%)
  blocking collectives  50 us (5%)
  between operations  16.6 us (2%)
    psum x2, waiting for transfers between devices, on_device(): lax.psum((grad_norm1, matmul(normed1_b.T, qg_b), matmul(normed1_b.T, kg_b...  290 us
    psum x1, waiting for transfers between devices, on_device(): lax.psum(gate_grad.astype(jnp.bfloat16), ('dp', 'seq')).astype(jnp.float32)  129 us
    another operation x5, other arithmetic, delta_run(): lax.linalg.triangular_solve(l_mat, right_side, left_side=True, lower=True...  60.9 us
    all_gather x1, waiting for transfers between devices, on_device(): lax.all_gather(value_grad.astype(jnp.bfloat16), ('dp', 'seq'))  56.1 us
    psum x1, waiting for transfers between devices, on_device(): lax.psum(normed2_part.astype(jnp.bfloat16), 'tensor').astype(jnp.float32)  40.5 us
    psum x1, waiting for transfers between devices, on_device(): lax.psum(matmul(gated_b, o_mat).astype(jnp.bfloat16), 'tensor')  40.1 us
    dot_general x30, matrix products, matmul(): return jnp.dot(left, right, preferred_element_type=jnp.float32)  39.8 us
    psum x1, blocking collectives, on_device(): lax.psum(input_grads[10].astype(jnp.bfloat16), ('dp', 'seq'))  30.4 us
  transfers between devices with their start and end apart: 11, of which 6 were waited for; matrix products, arithmetic and copies ran while one was open for 8% of the time, Pallas kernels for 0%

profile of v1, /device:TPU:0, one launch (start us, length us, event | category | flops | bytes accessed | tf_op | source)
XLA Modules:
  0.0 921.2 jit_solution(9460976850952864032)
XLA Ops:
  13.4 2.4 collective-permute-start
  27.3 59.7 %custom-call.11 = f32[6,2,1,64,64]{3,4,2,1,0:T(8,128)S(1)} custom-call(f32[6,2,1,64,64]{4,3,2,1,0:T(8,128)} %get-tuple-element.1081), custom_call_target="InvertDiagBlocksLowerTriangular" | custom-call | tf_op jit(solution)/shard_map/triangular_solve/custom-call.1 | solution.py:104
  88.0 2.1 fusion.103
  91.1 2.0 while.77
  93.8 1.9 collective-permute-start.1
  95.7 2.9 fusion.145
  101.3 1.9 copy.179
  103.2 2.7 bitcast_multiply_fusion.11
  109.4 9.7 %while.75 = (s32[]{:T(128)}, f32[6,128,64]{1,2,0:T(8,128)S(1)}, f32[2,6,64,64]{3,2,1,0:T(8,128)}, f32[2,6,128,64]{2,3,1,0:T(8,128)}, f32[2,6,64,64]{3,2,1,0:T(8,...) while((s32[]{:T(128)}, f32[6,128,64]{1,2,0:T(8,128)S(1)}, ...), condition=%wide.region_7.9_spmd, body=%wide.region_6.8_spmd.sunk | while | flops 132268032 | bytes 5707657 | solution.py:139
  119.7 1.9 copy.188
  122.8 10.7 %psum.161 = f32[128,6]{0,1:T(8,128)S(1)} all-reduce(f32[128,6]{0,1:T(8,128)S(1)} %fusion.174), channel_id=1, replica_groups=mesh['dp'=4,'seq'=2,'tensor'=4] {'tensor'}, use_global_device_ids=true, to_apply=%region_9.11 | all-reduce | flops 768 | bytes 6144 | tf_op jit(solution)/shard_map/psum | solution.py:217
  134.8 2.2 multiply_convert_fusion.3
  138.5 1.9 copy.193
  140.5 40.1 %all-reduce.39.cloned.1.call-done = bf16[128,1024]{1,0:T(8,128)(2,1)} async-done(((bf16[128,1024]{1,0:T(8,128)(2,1)}), bf16[128,1024]{1,0:T(8,128)(2,1)}) %all-reduce.39.cloned.1.call-update) | async-done | bytes 262160 | tf_op jit(solution)/shard_map/psum | solution.py:221
  183.0 2.0 fusion.242
  187.3 1.6 convolution_convert_fusion.1
  189.0 1.6 convolution_convert_fusion
  191.7 2.6 convolution_convert_fusion.6
  194.3 40.5 %all-reduce.41.cloned.1.call-done = bf16[128,1024]{1,0:T(8,128)(2,1)} async-done(((bf16[128,1024]{1,0:T(8,128)(2,1)}), bf16[128,1024]{1,0:T(8,128)(2,1)}) %all-reduce.41.cloned.1.call-update) | async-done | bytes 262160 | tf_op jit(solution)/shard_map/psum | solution.py:241
  234.9 1.9 fusion.120
  239.0 1.7 multiply_reduce_fusion.14
  241.3 8.9 psum.165
  253.3 8.5 while.78
  263.1 2.3 convolution_bitcast_fusion.4
  269.4 20.2 %while.76 = (s32[]{:T(128)}, f32[6,128,64]{1,2,0:T(8,128)S(1)}, f32[2,6,64,64]{3,2,1,0:T(8,128)}, f32[2,6,64,128]{3,2,1,0:T(8,128)}, f32[2,6,64,128]{3,2,0,1:T(8...) while((s32[]{:T(128)}, f32[6,128,64]{1,2,0:T(8,128)S(1)}, ...), condition=%wide.region_21.23_spmd, body=%wide.region_19.22_spmd.sunk | while | flops 264560640 | bytes 16820268 | solution.py:139
  270.5 1.9 fusion.394
  276.5 1.6 fusion.392
  280.5 1.9 fusion.394
  286.5 1.6 fusion.392
  290.1 2.3 fusion.111
  294.9 2.4 multiply_reduce_fusion.10
  301.7 1.5 add_add_fusion.2
  303.2 2.0 copy.214
  305.2 1.7 convolution_add_fusion.17
  308.9 1.8 add_add_fusion.3
  312.0 2.6 multiply_reduce_fusion.3
  320.8 2.1 multiply_reduce_fusion.17
  326.5 1.8 fusion.229
  332.4 1.5 add_add_fusion.4
  335.9 4.0 reduce_window_sum.25
  340.0 2.1 fusion.231
  343.4 1.7 split.35
  345.0 1.7 split.32
  348.2 1.5 scatter-add.11
  349.6 2.4 fusion.247
  353.4 2.6 convolution_add_fusion.13
  358.1 1.8 fusion.94
  362.3 1.6 convolution_convert_fusion.2
  372.1 2.3 fusion.248
  374.4 2.3 fusion.246
  377.5 30.4 %all-reduce.29 = (bf16[4,6,64]{2,1,0:T(8,128)(2,1)S(1)}, bf16[64]{0:T(256)(128)(2,1)S(1)}, bf16[1024]{0:T(1024)(128)(2,1)S(1)}) all-reduce(bf16[4,6,64]{2,1,0:T(8,128)(2,1)S(1)} %convert_element_type.201, bf16[64]{0:T(256)(128)(2,1)S(1)} %copy-done.180, ...), channel_id=1, replica_groups=mesh['dp'=4,'seq'=2,'tensor'=4] {'dp','seq'}, use_global_device_ids=true, to_apply=%region_57.59 | all-reduce | flops 2624 | bytes 10496 | tf_op jit(solution)/shard_map/psum | solution.py:301
  409.7 1.8 add_convert_fusion
  411.4 1.8 convert_add_fusion.1
  413.2 128.9 %all-reduce.47.cloned.1.call-done = (bf16[1024,6,64]{0,2,1:T(8,128)(2,1)}, bf16[6,64,1024]{2,1,0:T(8,128)(2,1)}, bf16[1024,704]{0,1:T(8,128)(2,1)}, bf16[1024,704]{0,1:T(8,128)(2,1)}, bf16[704,1024]{1,0:T(8,128)(2,1)}) async-done(((bf16[1024,6,64]{0,2,1:T(8,128)(2,1)}, bf16[6,64,1024]{2,1,0:T(8,128)(2,1)}, bf16[1024,704]{0,1:T(8,128)(2,1)}, bf16[1024,704]{0,1:T(8,128)(2,1)}, bf16[704,1024]{1,0:T(8,128)(2,1)}), ...) | async-done | bytes 5898256 | tf_op jit(solution)/shard_map/psum | solution.py:300
  542.1 2.5 convert_element_type.199
  546.6 1.9 convert_element_type.210
  548.5 1.9 convert_element_type.212
  550.5 1.9 convert_element_type.214
  552.4 56.1 %all-gather.2.cloned.1.call-done = bf16[8,1024,6,64]{1,3,2,0:T(8,128)(2,1)} async-done(((bf16[1,1024,6,64]{1,3,2,0:T(8,128)(2,1)}), bf16[8,1024,6,64]{1,3,2,0:T(8,128)(2,1)}) %all-gather.2.cloned.1.call-update) | async-done | bytes 6291472 | tf_op jit(solution)/shard_map/all_gather | solution.py:297
  608.4 4.4 reduce_sum.374
  614.1 126.1 %all-reduce.43.cloned.1.call-done = (f32[1024]{0:T(1024)}, f32[1024,6]{0,1:T(8,128)}, f32[1024,6]{0,1:T(8,128)}, f32[4,768]{1,0:T(4,128)}, f32[4,768]{1,0:T(4,128)}, /*index=5*/f32[6]{0:T(128)}, f32[6]{0:T(128)}) async-done(((f32[1024]{0:T(1024)}, f32[1024,6]{0,1:T(8,128)}, f32[1024,6]{0,1:T(8,128)}, f32[4,768]{1,0:T(4,128)}, f32[4,768]{1,0:T(4,128)}, /*index=5*/f32[6]{0:T(128)}, f32[6]{0:T(128)}), ...) | async-done | bytes 77888 | tf_op jit(solution)/shard_map/psum | solution.py:280
  740.2 163.5 %all-reduce.45.cloned.1.call-done = (f32[1024,768]{1,0:T(8,128)}, f32[1024,768]{1,0:T(8,128)}) async-done(((f32[1024,768]{1,0:T(8,128)}, f32[1024,768]{1,0:T(8,128)}), (f32[1024,768]{1,0:T(8,128)}, f32[1024,768]{1,0:T(8,128)})) %all-reduce.45.cloned.1.call-update) | async-done | bytes 6291472 | tf_op jit(solution)/shard_map/psum | solution.py:280
  905.0 3.9 copy.410
  909.0 1.7 copy.411
  (649 shorter events, 132.8 us)
Async XLA Ops:
  7.2 173.4 %all-reduce.39.cloned.1.call-start = ((), (), s32[]{:S(2)}) async-start(), calls=%async_computation | async-start | bytes 524288 | tf_op jit(solution)/shard_map/psum | solution.py:221
  10.6 7.7 copy-start.1
  11.0 10.9 %copy-start.39 = (f32[128,768]{1,0:T(8,128)}, f32[128,768]{1,0:T(8,128)S(1)}, u32[]{:S(2)}) copy-start(f32[128,768]{1,0:T(8,128)S(1)} %fusion.239) | copy-start | bytes 1179652
  11.1 4.8 copy-start.183
  11.1 4.9 copy-start.147
  11.1 4.9 copy-start.184
  11.5 13.4 %copy-start.70 = (f32[128,384]{1,0:T(8,128)}, f32[128,384]{1,0:T(8,128)S(1)}, u32[]{:S(2)}) copy-start(f32[128,384]{1,0:T(8,128)S(1)} %fusion.240) | copy-start | bytes 589828
  11.5 6.8 copy-start.104
  11.5 7.3 copy-start.159
  11.5 7.4 copy-start.160
  12.3 6.7 copy-start.161
  13.4 7.9 collective-permute-start
  18.5 5.4 copy-start.130
  18.6 7.5 copy-start.91
  18.8 5.1 copy-start.120
  18.8 5.1 copy-start.122
  18.9 5.1 copy-start.124
  18.9 5.1 copy-start.126
  19.0 7.1 copy-start.100
  20.3 5.7 copy-start.102
  26.1 61.9 %copy-start.45 = (f32[6,128,64]{2,1,0:T(8,128)}, f32[6,128,64]{2,1,0:T(8,128)S(1)}, u32[]{:S(2)}) copy-start(f32[6,128,64]{2,1,0:T(8,128)S(1)} %copy.172) | copy-start | bytes 589828
  91.1 4.6 copy-start.98
  91.1 4.6 copy-start.112
  91.1 4.6 copy-start.114
  91.1 4.6 copy-start.116
  91.1 4.6 copy-start.118
  93.8 13.1 %collective-permute-start.1 = (bf16[6,128,64]{1,2,0:T(8,128)(2,1)}, bf16[6,128,64]{1,2,0:T(8,128)(2,1)}, u32[]{:S(2)}, u32[]{:S(2)}) collective-permute-start(bf16[6,128,64]{1,2,0:T(8,128)(2,1)} %convert_element_type.168), channel_id=1, source_target_pairs={{0,4},{1,5},{2,6},{3,7},{8,12},{9,13},{10,14},{11,15},{16,20},{17,... | collective-permute-start | bytes 294920 | tf_op jit(solution)/shard_map/ppermute | solution.py:15
  99.8 6.1 copy-start.10
  119.1 15.7 %copy-start.2 = (bf16[128,1024]{1,0:T(8,128)(2,1)S(1)}, bf16[128,1024]{1,0:T(8,128)(2,1)}, u32[]{:S(2)}) copy-start(bf16[128,1024]{1,0:T(8,128)(2,1)} %copy-done.1) | copy-start | bytes 786436
  119.1 15.7 %copy-start.181 = (f32[64]{0:T(128)S(1)}, f32[64]{0:T(128)}, u32[]{:S(2)}) copy-start(f32[64]{0:T(128)} %param.49) | copy-start | bytes 772
  137.0 46.0 %copy-start.87 = (bf16[128,6,64]{0,2,1:T(8,128)(2,1)}, bf16[128,6,64]{0,2,1:T(8,128)(2,1)S(1)}, u32[]{:S(2)}) copy-start(bf16[128,6,64]{0,2,1:T(8,128)(2,1)S(1)} %get-tuple-element.1093) | copy-start | bytes 294916
  137.0 43.6 %copy-start.4 = (bf16[128,1024]{1,0:T(8,128)(2,1)S(1)}, bf16[128,1024]{1,0:T(8,128)(2,1)}, u32[]{:S(2)}) copy-start(bf16[128,1024]{1,0:T(8,128)(2,1)} %param.36) | copy-start | bytes 786436
  137.0 44.9 %copy-start.110 = (f32[1024]{0:T(1024)S(1)}, f32[1024]{0:T(1024)}, u32[]{:S(2)}) copy-start(f32[1024]{0:T(1024)} %param.51) | copy-start | bytes 12292
  138.0 96.8 %all-reduce.41.cloned.1.call-start = ((), (), s32[]{:S(2)}) async-start(), calls=%async_computation.1 | async-start | bytes 524288 | tf_op jit(solution)/shard_map/psum | solution.py:241
  180.6 4.4 copy-start.34
  191.7 218.0 %all-reduce.49.cloned.1.call-start = ((), (), s32[]{:S(2)}) async-start(), calls=%async_computation.6 | async-start | bytes 1048576 | tf_op jit(solution)/shard_map/psum | solution.py:229
  238.2 12.0 %copy-start.95 = (f32[128,6,64]{0,2,1:T(8,128)S(1)}, f32[128,6,64]{0,2,1:T(8,128)}, u32[]{:S(2)}) copy-start(f32[128,6,64]{0,2,1:T(8,128)} %get-tuple-element.1094) | copy-start | bytes 589828
  253.3 9.9 %copy-start.89 = (bf16[128,6,64]{0,2,1:T(8,128)(2,1)S(1)}, bf16[128,6,64]{0,2,1:T(8,128)(2,1)}, u32[]{:S(2)}) copy-start(bf16[128,6,64]{0,2,1:T(8,128)(2,1)} %get-tuple-element.1054) | copy-start | bytes 294916
  261.8 3.6 collective-permute-start.2
  269.4 4.9 copy-start.6
  269.4 4.9 copy-start.54
  279.4 4.8 copy-start.6
  279.4 4.9 copy-start.54
  303.2 4.6 copy-start.11
  307.8 4.1 copy-start.40
  307.8 4.1 copy-start.42
  320.8 7.5 copy-start.97
  320.8 7.5 copy-start.108
  320.8 11.6 %copy-start.93 = (f32[6,2,64]{2,1,0:T(2,128)S(1)}, f32[6,2,64]{2,1,0:T(2,128)}, u32[]{:S(2)}) copy-start(f32[6,2,64]{2,1,0:T(2,128)} %copy-done.91) | copy-start | bytes 9220
  323.7 23.7 %copy-start.19 = (f32[128,768]{1,0:T(8,128)S(1)}, f32[128,768]{1,0:T(8,128)}, u32[]{:S(2)}) copy-start(f32[128,768]{1,0:T(8,128)} %copy-done.18) | copy-start | bytes 1179652
  323.7 23.7 %copy-start.21 = (f32[128,768]{1,0:T(8,128)S(1)}, f32[128,768]{1,0:T(8,128)}, u32[]{:S(2)}) copy-start(f32[128,768]{1,0:T(8,128)} %copy-done.20) | copy-start | bytes 1179652
  325.2 22.2 %collective-permute-start.3 = (f32[3,1920]{1,0:T(4,128)}, f32[3,1920]{1,0:T(4,128)}, u32[]{:S(2)}, u32[]{:S(2)}) collective-permute-start(f32[3,1920]{1,0:T(4,128)} %pad_maximum_fusion.4), channel_id=1, source_target_pairs={{4,0},{5,1},{6,2},{7,3},{12,8},{13,9},{14,10},{15,11},{20,16},{21,... | collective-permute-start | bytes 69128 | tf_op jit(solution)/shard_map/ppermute | solution.py:15
  340.0 7.4 copy-start.23
  340.0 7.4 copy-start.25
  340.0 7.4 copy-start.27
  348.2 5.2 copy-start.29
  362.2 179.9 %all-reduce.47.cloned.1.call-start = ((), (), s32[]{:S(2)}) async-start(), calls=%async_computation.5 | async-start | bytes 11796480 | tf_op jit(solution)/shard_map/psum | solution.py:300
  366.5 5.6 copy-start.72
  366.5 242.0 %all-gather.2.cloned.1.call-start = ((), (), s32[]{:S(2)}) async-start(), calls=%async_computation.2 | async-start | bytes 7077888 | tf_op jit(solution)/shard_map/all_gather | solution.py:297
  368.6 371.6 %all-reduce.43.cloned.1.call-start = ((), (), s32[]{:S(2)}) async-start(), calls=%async_computation.3 | async-start | bytes 190464 | tf_op jit(solution)/shard_map/psum | solution.py:280
  374.4 529.4 %all-reduce.45.cloned.1.call-start = ((), (), s32[]{:S(2)}) async-start(), calls=%async_computation.4 | async-start | bytes 12582912 | tf_op jit(solution)/shard_map/psum | solution.py:280
  376.7 32.9 %copy-start.17 = (bf16[128,1024]{1,0:T(8,128)(2,1)S(1)}, bf16[128,1024]{1,0:T(8,128)(2,1)}, u32[]{:S(2)}) copy-start(bf16[128,1024]{1,0:T(8,128)(2,1)} %all-reduce.39.cloned.1.call-done) | copy-start | bytes 786436
  909.0 4.1 copy-start.186
  909.0 4.6 copy-start.185
  (153 other events, 358.4 us)
Sparse Core Ops, SparseCore 0:
  138.1 42.4 all-reduce.38
  191.8 42.9 all-reduce.40
  362.3 46.7 all-reduce.48
  413.4 128.6 all-reduce.46
  543.6 64.8 all-gather.1
  615.9 124.3 all-reduce.42
  746.6 157.1 all-reduce.44
